TPU v7x, 256 devices: a whole 4x4x8 slice. The times are simulated.
256 devices in a mesh: enc: 8 (over z), kr: 8 (over x_lo, y), kc: 4 (over x_hi, core).
Axes of the slice: x: 4 (x_hi: 2, x_lo: 2; x = x_hi * 2 + x_lo), y: 4, z: 8, core: 2. Of those that a mesh axis runs over, the one named last changes fastest.
Arguments:
- inputs: bfloat16 [49152, 1024], P(('enc', 'kr', 'kc')), may hold values from -24 to 24
- w_first: bfloat16 [1024, 1024], replicated, may hold values from -0.1875 to 0.1875
- w_second: bfloat16 [1024, 64], replicated, may hold values from -0.1875 to 0.1875
- inv_length: float32 [64], replicated, may hold values from 0.05 to 1.8
- probes: bfloat16 [49152, 128], P(('enc', 'kr', 'kc')), may hold values from -6 to 6
- solves: bfloat16 [49152, 128], P(('enc', 'kr', 'kc')), may hold values from -6 to 6
Outputs:
- products: bfloat16 [49152, 128], P(('enc', 'kr', 'kc'))
- grad_first: float32 [1024, 1024], P(('enc', 'kr', 'kc'))
- grad_second: float32 [1024, 64], P(('enc', 'kr', 'kc'))
All inputs are finite; a program needn't handle non-finite values.
Results may differ from a plain program's by a relative error of at most 0.007.
The roundings to bfloat16 on the way count: a program that leaves them out, or rounds other values in their place, can miss the bound.
Values may be sent and summed in bfloat16 or wider, within the bound.
A program may use at most 64 MiB of HBM per device.

v0:
```python
import math
import jax
import jax.numpy as jnp
from jax import lax
from jax.sharding import PartitionSpec as P

probe_gain = 0.5
loss_gain = 0.02


def contract_inner(left, right):
    return lax.dot_general(
        left, right, (((1,), (1,)), ((), ())), preferred_element_type=jnp.float32
    )


def contract_outer(left, right):
    return lax.dot_general(
        left, right, (((0,), (0,)), ((), ())), preferred_element_type=jnp.float32
    )


def kernel_tile(row_feat, row_norm, col_feat):
    col_wide = col_feat.astype(jnp.float32)
    col_norm = jnp.sum(col_wide * col_wide, axis=1)
    cross = contract_inner(row_feat, col_feat)
    return jnp.exp(-0.5 * (row_norm[:, None] + col_norm[None, :] - 2.0 * cross))


def split_blocks(array):
    length = array.shape[0]
    candidates = [
        option_width
        for option_width in (1024, 768, 512, 384, 256, 192, 128)
        if length % option_width == 0
    ]
    width = candidates[0]
    return array.reshape(length // width, width, array.shape[1])


def row_totals(parts):
    return (
        lax.psum_scatter(parts[0], "kc", scatter_dimension=0, tiled=True),
        lax.psum_scatter(parts[1], "kc", scatter_dimension=0, tiled=True),
        lax.psum_scatter(parts[2], "kc", scatter_dimension=0, tiled=True),
    )


def local(inputs, w_first, w_second, inv_length, probes, solves):
    pre = jnp.dot(inputs, w_first, preferred_element_type=jnp.float32)
    hidden = jax.nn.silu(pre).astype(jnp.bfloat16)
    features = jnp.dot(hidden, w_second, preferred_element_type=jnp.float32)
    scaled = (features * inv_length[None, :]).astype(jnp.bfloat16)
    own_wide = scaled.astype(jnp.float32)
    own_rows = inputs.shape[0]
    row_count = own_rows * lax.axis_size("kc")
    feat_width = scaled.shape[1]
    probe_width = probes.shape[1]
    zeros_init = (
        jnp.zeros((row_count, probe_width), jnp.float32),
        jnp.zeros((row_count, feat_width), jnp.float32),
        jnp.zeros((row_count,), jnp.float32),
    )
    row_feat, row_probe, row_solve = (
        lax.all_gather(scaled, "kc", axis=0, tiled=True),
        lax.all_gather(probes, "kc", axis=0, tiled=True),
        lax.all_gather(solves, "kc", axis=0, tiled=True),
    )
    row_wide = row_feat.astype(jnp.float32)
    row_norm = jnp.sum(row_wide * row_wide, axis=1)
    portion = (
        lax.all_gather(scaled, ("enc", "kr"), axis=0, tiled=True),
        lax.all_gather(probes, ("enc", "kr"), axis=0, tiled=True),
        lax.all_gather(solves, ("enc", "kr"), axis=0, tiled=True),
    )

    def advance(totals, columns):
        col_feat, col_probe, col_solve = columns
        kernel = kernel_tile(row_feat, row_norm, col_feat)
        first = kernel * contract_inner(row_solve, col_probe)
        second = kernel * contract_inner(row_probe, col_solve)
        mixed_part = jnp.dot(
            first.astype(jnp.bfloat16), col_feat, preferred_element_type=jnp.float32
        ) + jnp.dot(second.astype(jnp.bfloat16), col_feat, preferred_element_type=jnp.float32)
        vpart = jnp.dot(kernel.astype(jnp.bfloat16), col_probe, preferred_element_type=jnp.float32)
        return (
            (
                totals[0] + vpart,
                totals[1] + mixed_part,
                totals[2] + jnp.sum(first, axis=1) + jnp.sum(second, axis=1),
            ),
            None,
        )

    stacked = tuple((split_blocks(item) for item in portion))
    result, _ = lax.scan(advance, zeros_init, stacked)
    vsum, mixed, sums = row_totals(result)
    products = (vsum * probe_gain).astype(jnp.bfloat16)
    lscale = loss_gain / math.sqrt(probe_width)
    dfeat = -lscale * inv_length[None, :] * (sums[:, None] * own_wide - mixed)
    dfeat_half = dfeat.astype(jnp.bfloat16)
    second_term = contract_outer(hidden, dfeat_half)
    back_hidden = contract_inner(dfeat_half, w_second)
    sigma = jax.nn.sigmoid(pre)
    dpre = (back_hidden * sigma * (1.0 + pre * (1.0 - sigma))).astype(jnp.bfloat16)
    first_term = contract_outer(inputs, dpre)
    grad_first, grad_second = (
        lax.psum_scatter(first_term, ("enc", "kr", "kc"), scatter_dimension=0, tiled=True),
        lax.psum_scatter(second_term, ("enc", "kr", "kc"), scatter_dimension=0, tiled=True),
    )
    return (products, grad_first, grad_second)


def solution(mesh):
    in_specs = (
        P(("enc", "kr", "kc"), None),
        P(),
        P(),
        P(),
        P(("enc", "kr", "kc"), None),
        P(("enc", "kr", "kc"), None),
    )
    out_specs = (
        P(("enc", "kr", "kc"), None),
        P(("enc", "kr", "kc"), None),
        P(("enc", "kr", "kc"), None),
    )
    return jax.shard_map(local, mesh=mesh, in_specs=in_specs, out_specs=out_specs, check_vma=False)
```

profile of v0, /device:TPU:97, one launch (start us, length us, event | category | flops | bytes accessed | tf_op | source)
XLA Modules:
  0.0 1431.5 jit_solution(13192146417634224073)
XLA Ops:
  7.2 1.5 copy-done
  8.8 2.5 multiply_convert_fusion
  13.8 7.6 all-gather
  23.1 7.3 all_gather.21
  30.4 7.4 all_gather.23
  38.7 217.8 %all-gather.10.cloned.1.call-done = bf16[64,192,64]{1,2,0:T(8,128)(2,1)} async-done(((bf16[1,192,64]{1,2,0:T(8,128)(2,1)}), bf16[64,192,64]{1,2,0:T(8,128)(2,1)}) %all-gather.10.cloned.1.call-update) | async-done | bytes 1572880 | tf_op jit(solution)/shard_map/all_gather | solution.py:72
  256.5 4.6 copy.20
  261.1 295.6 %all-gather.6.cloned.1.call-done = bf16[12288,128]{1,0:T(8,128)(2,1)} async-done(((bf16[192,128]{1,0:T(8,128)(2,1)}), bf16[12288,128]{1,0:T(8,128)(2,1)}) %all-gather.6.cloned.1.call-update) | async-done | bytes 3145744 | tf_op jit(solution)/shard_map/all_gather | solution.py:73
  556.7 300.3 %all-gather.8.cloned.1.call-done = bf16[12288,128]{1,0:T(8,128)(2,1)} async-done(((bf16[192,128]{1,0:T(8,128)(2,1)}), bf16[12288,128]{1,0:T(8,128)(2,1)}) %all-gather.8.cloned.1.call-update) | async-done | bytes 3145744 | tf_op jit(solution)/shard_map/all_gather | solution.py:74
  857.0 162.3 %while.15 = (s32[]{:T(128)}, f32[768,128]{1,0:T(8,128)S(1)}, f32[768,64]{0,1:T(8,128)S(1)}, f32[768]{0:T(1024)S(1)}, f32[768]{0:T(1024)S(1)}, /*index=5*/bf16[12...) while((s32[]{:T(128)}, f32[768,128]{1,0:T(8,128)S(1)}, ...), condition=%wide.region_5.6_spmd.clone, body=%wide.region_1.5_spmd.clone.sunk | while | flops 915160832 | bytes 35353800 | solution.py:96
  858.2 3.5 fusion.88
  861.6 2.7 fusion.89
  864.5 1.5 fusion.90
  867.5 1.5 fusion.92
  871.7 3.5 fusion.88
  875.2 2.7 fusion.89
  878.1 1.5 fusion.90
  881.0 1.5 fusion.92
  885.2 3.5 fusion.88
  888.7 2.7 fusion.89
  891.6 1.5 fusion.90
  894.5 1.5 fusion.92
  898.7 3.5 fusion.88
  902.2 2.7 fusion.89
  905.1 1.5 fusion.90
  908.1 1.5 fusion.92
  912.3 3.5 fusion.88
  915.7 2.7 fusion.89
  918.6 1.5 fusion.90
  921.6 1.5 fusion.92
  925.8 3.5 fusion.88
  929.2 2.7 fusion.89
  932.2 1.5 fusion.90
  935.1 1.5 fusion.92
  939.3 3.5 fusion.88
  942.8 2.7 fusion.89
  945.7 1.5 fusion.90
  948.6 1.5 fusion.92
  952.8 3.5 fusion.88
  956.3 2.7 fusion.89
  959.2 1.5 fusion.90
  962.2 1.5 fusion.92
  966.3 3.5 fusion.88
  969.8 2.7 fusion.89
  972.7 1.5 fusion.90
  975.7 1.5 fusion.92
  979.9 3.5 fusion.88
  983.3 2.7 fusion.89
  986.3 1.5 fusion.90
  989.2 1.5 fusion.92
  993.4 3.5 fusion.88
  996.9 2.7 fusion.89
  999.8 1.5 fusion.90
  1002.7 1.5 fusion.92
  1006.9 3.5 fusion.88
  1010.4 2.7 fusion.89
  1013.3 1.5 fusion.90
  1016.2 1.5 fusion.92
  1021.5 53.3 %all-reduce = f32[768]{0:T(1024)S(1)} all-reduce(f32[768]{0:T(1024)S(1)} %get-tuple-element.63), channel_id=3, replica_groups=mesh['enc'=8,'kr'=8,'kc'=4] {'kc'}, use_global_device_ids=true, to_apply=%region_7.8.clone | all-reduce | flops 768 | bytes 6144
  1075.0 33.0 %reduce-scatter.8.cloned.1.call-done = f32[192,64]{1,0:T(8,128)} async-done(((f32[768,64]{1,0:T(8,128)}), f32[192,64]{1,0:T(8,128)}) %reduce-scatter.8.cloned.1.call-update) | async-done | bytes 49168
  1110.3 4.2 convolution_bitcast_fusion
  1114.6 28.4 %reduce-scatter.6.cloned.1.call-done = f32[192,128]{1,0:T(8,128)} async-done(((f32[768,128]{1,0:T(8,128)}), f32[192,128]{1,0:T(8,128)}) %reduce-scatter.6.cloned.1.call-update) | async-done | bytes 98320 | tf_op jit(solution)/shard_map/reduce_scatter | solution.py:43
  1143.0 1.5 multiply_convert_fusion.1
  1144.5 276.8 %all-reduce.6.cloned.1.call-done = (f32[1024,1024]{0,1:T(8,128)}, f32[1024,64]{1,0:T(8,128)}) async-done(((f32[1024,1024]{0,1:T(8,128)}, f32[1024,64]{1,0:T(8,128)}), (f32[1024,1024]{0,1:T(8,128)}, f32[1024,64]{1,0:T(8,128)})) %all-reduce.6.cloned.1.call-update) | async-done | bytes 4456464
  (117 shorter events, 62.3 us)
Async XLA Ops:
  7.2 1.6 copy-start
  7.2 4.1 copy-start.6
  7.2 4.1 copy-start.7
  7.2 249.3 %all-gather.10.cloned.1.call-start = ((), (), s32[]{:S(2)}) async-start(), calls=%async_computation.5 | async-start | bytes 2129920 | tf_op jit(solution)/shard_map/all_gather | solution.py:72
  8.8 21.6 %copy-start.5 = (bf16[192,128]{1,0:T(8,128)(2,1)S(1)}, bf16[192,128]{1,0:T(8,128)(2,1)}, u32[]{:S(2)}) copy-start(bf16[192,128]{1,0:T(8,128)(2,1)} %param.12) | copy-start | bytes 147460
  12.2 544.5 %all-gather.6.cloned.1.call-start = ((), (), s32[]{:S(2)}) async-start(), calls=%async_computation.2 | async-start | bytes 3194880 | tf_op jit(solution)/shard_map/all_gather | solution.py:73
  13.0 844.0 %all-gather.8.cloned.1.call-start = ((), (), s32[]{:S(2)}) async-start(), calls=%async_computation.3 | async-start | bytes 3194880 | tf_op jit(solution)/shard_map/all_gather | solution.py:74
  13.7 1094.4 %reduce-scatter.8.cloned.1.call-start = ((), (), s32[]{:S(2)}) async-start(), calls=%async_computation.6 | async-start | bytes 491520
  21.7 0.6 copy-start.3
  857.0 163.3 %copy-start.8 = (u32[256]{0:T(256)S(1)}, u32[256]{0:T(256)}, u32[]{:S(2)}) copy-start(u32[256]{0:T(256)} %constant.36) | copy-start | bytes 3076
  857.0 252.1 %copy-start.4 = (bf16[192,64]{0,1:T(8,128)(2,1)S(1)}, bf16[192,64]{0,1:T(8,128)(2,1)}, u32[]{:S(2)}) copy-start(bf16[192,64]{0,1:T(8,128)(2,1)} %fusion.38) | copy-start | bytes 73732
  861.6 2.9 copy-start.1
  875.2 2.9 copy-start.1
  888.7 2.9 copy-start.1
  902.2 2.9 copy-start.1
  915.7 2.9 copy-start.1
  929.2 2.9 copy-start.1
  942.8 2.9 copy-start.1
  956.3 2.9 copy-start.1
  969.8 2.9 copy-start.1
  983.3 2.9 copy-start.1
  996.9 2.9 copy-start.1
  1010.4 2.9 copy-start.1
  1019.3 55.6 %copy-start.2 = (f32[768,128]{1,0:T(8,128)}, f32[768,128]{1,0:T(8,128)S(1)}, u32[]{:S(2)}) copy-start(f32[768,128]{1,0:T(8,128)S(1)} %get-tuple-element.62) | copy-start | bytes 1179652
  1020.2 122.8 %reduce-scatter.6.cloned.1.call-start = ((), (), s32[]{:S(2)}) async-start(), calls=%async_computation.4 | async-start | bytes 491520 | tf_op jit(solution)/shard_map/reduce_scatter | solution.py:43
  1074.9 346.5 %all-reduce.6.cloned.1.call-start = ((), (), s32[]{:S(2)}) async-start(), calls=%async_computation.7 | async-start | bytes 9437184
Sparse Core Ops, SparseCore 0:
  12.3 244.0 all-gather.9
  258.3 298.3 all-gather.5
  558.5 298.4 all-gather.7
  1020.3 87.6 reduce-scatter.7
  1110.7 32.2 reduce-scatter.5
  1148.4 272.9 all-reduce.5
where the time goes:
time: 1430 us
  waiting for transfers between devices  1150 us (80%)
  matrix products  154 us (11%)
  blocking collectives  75.6 us (5%)
  other arithmetic  16.6 us (1%)
  local copies, waits for them, and re-layouts  15.8 us (1%)
  between operations  14.9 us (1%)
    unnamed x8, waiting for transfers between devices  311 us
    all_gather x1, waiting for transfers between devices, local(): lax.all_gather(solves, ('enc', 'kr'), axis=0, tiled=True)  300 us
    all_gather x1, waiting for transfers between devices, local(): lax.all_gather(probes, ('enc', 'kr'), axis=0, tiled=True)  296 us
    all_gather x1, waiting for transfers between devices, local(): lax.all_gather(scaled, ('enc', 'kr'), axis=0, tiled=True)  218 us
    dot_general x36, matrix products, contract_inner(): lax.dot_general(left, right, (((1,), (1,)), ((), ())), preferred_element_...  78.7 us
    unnamed x1, blocking collectives  53.3 us
    dot_general x12, matrix products, advance(): jnp.dot(kernel.astype(jnp.bfloat16), col_probe, preferred_element_type=jn...  32.7 us
  transfers between devices with their start and end apart: 6, of which 6 were waited for; matrix products, arithmetic and copies ran while one was open for 1% of the time, Pallas kernels for 0%

commit v1 on v0

--- a/solution.py
+++ b/solution.py
@@ -70,7 +70,10 @@
     row_norm = jnp.sum(row_wide * row_wide, axis=1)
     portion = (
         lax.all_gather(scaled, ("enc", "kr"), axis=0, tiled=True),
-        lax.all_gather(probes, ("enc", "kr"), axis=0, tiled=True),
+        jnp.concatenate(
+            lax.all_to_all(jnp.stack([probes] * lax.axis_size(("enc", "kr"))), ("enc", "kr"), 0, 0),
+            axis=0,
+        ),
         lax.all_gather(solves, ("enc", "kr"), axis=0, tiled=True),
     )
 

time: 1430 us -> 1150 us (0.80)
  waiting for transfers between devices: 1150 us -> 837 us
    all_gather x1 -> x0, waiting for transfers between devices: 296 us -> none  [local(): lax.all_gather(probes, ('enc', 'kr'), axis=0, tiled=True)]
    unnamed x8 -> x7, waiting for transfers between devices: 311 us -> 311 us
  transfers between devices with their start and end apart: 6 -> 6, of which waited for: 6 -> 5; matrix products, arithmetic and copies ran while one was open for 1% -> 2% of each run, Pallas kernels for 0% -> 0%
where the time goes in v1:
time: 1150 us; the launch traced here: 1140 us
  waiting for transfers between devices  837 us (73%)
  matrix products  154 us (13%)
  blocking collectives  84.6 us (7%)
  local copies, waits for them, and re-layouts  25.3 us (2%)
  other arithmetic  16.5 us (1%)
  between operations  14.6 us (1%)
  starting transfers between devices  11.8 us (1%)
    unnamed x7, waiting for transfers between devices  311 us
    all_gather x1, waiting for transfers between devices, local(): lax.all_gather(solves, ('enc', 'kr'), axis=0, tiled=True)  291 us
    all_gather x1, waiting for transfers between devices, local(): lax.all_gather(scaled, ('enc', 'kr'), axis=0, tiled=True)  206 us
    dot_general x36, matrix products, contract_inner(): lax.dot_general(left, right, (((1,), (1,)), ((), ())), preferred_element_...  78.6 us
    unnamed x1, blocking collectives  53.4 us
    dot_general x12, matrix products, advance(): jnp.dot(kernel.astype(jnp.bfloat16), col_probe, preferred_element_type=jn...  32.7 us
    reduce_scatter x1, waiting for transfers between devices, row_totals(): lax.psum_scatter(parts[0], 'kc', scatter_dimension=0, tiled=True)  28.4 us
  transfers between devices with their start and end apart: 6, of which 5 were waited for; matrix products, arithmetic and copies ran while one was open for 2% of the time, Pallas kernels for 0%

profile of v1, /device:TPU:97, one launch (start us, length us, event | category | flops | bytes accessed | tf_op | source)
XLA Modules:
  0.0 1144.5 jit_solution(8856312092959807326)
XLA Ops:
  8.8 2.5 multiply_convert_fusion
  12.2 2.4 stack.2
  14.6 11.6 %all-to-all-start = ((bf16[64,192,128]{2,1,0:T(8,128)(2,1)}), bf16[64,192,128]{2,1,0:T(8,128)(2,1)}, u32[]{:S(2)}, u32[]{:S(2)}) async-start(bf16[64,192,128]{2,1,0:T(8,128)(2,1)} %stack.2), calls=%async_computation | async-start | bytes 6291456 | tf_op jit(solution)/shard_map/all_to_all | solution.py:74
  27.0 12.8 %all-gather = bf16[4,192,64]{1,2,0:T(8,128)(2,1)S(1)} all-gather(bf16[1,192,64]{1,2,0:T(8,128)(2,1)S(1)} %bitcast.85), channel_id=1, replica_groups=mesh['enc'=8,'kr'=8,'kc'=4] {'kc'}, dimensions={0}, use_global_device_ids=true | all-gather | bytes 122880 | tf_op jit(solution)/shard_map/all_gather | solution.py:65
  41.5 8.7 all_gather.17
  50.3 9.5 all_gather.19
  60.7 206.3 %all-gather.7.cloned.1.call-done = bf16[64,192,64]{1,2,0:T(8,128)(2,1)} async-done(((bf16[1,192,64]{1,2,0:T(8,128)(2,1)}), bf16[64,192,64]{1,2,0:T(8,128)(2,1)}) %all-gather.7.cloned.1.call-update) | async-done | bytes 1572880 | tf_op jit(solution)/shard_map/all_gather | solution.py:72
  267.1 4.6 copy.20
  271.6 291.4 %all-gather.5.cloned.1.call-done = bf16[12288,128]{1,0:T(8,128)(2,1)} async-done(((bf16[192,128]{1,0:T(8,128)(2,1)}), bf16[12288,128]{1,0:T(8,128)(2,1)}) %all-gather.5.cloned.1.call-update) | async-done | bytes 3145744 | tf_op jit(solution)/shard_map/all_gather | solution.py:77
  563.1 169.4 %while.15 = (s32[]{:T(128)}, f32[768,128]{1,0:T(8,128)S(1)}, f32[768,64]{0,1:T(8,128)S(1)}, f32[768]{0:T(1024)}, f32[768]{0:T(1024)S(1)}, /*index=5*/bf16[12,102...) while((s32[]{:T(128)}, f32[768,128]{1,0:T(8,128)S(1)}, ...), condition=%wide.region_5.6_spmd.clone, body=%wide.region_1.5_spmd.clone.sunk | while | flops 915160832 | bytes 35378432 | solution.py:99
  564.2 3.5 fusion.88
  567.7 2.7 fusion.89
  570.6 1.5 fusion.90
  573.6 1.6 fusion.92
  578.4 3.5 fusion.88
  581.8 2.7 fusion.89
  584.7 1.5 fusion.90
  587.7 1.6 fusion.92
  592.5 3.5 fusion.88
  595.9 2.7 fusion.89
  598.8 1.5 fusion.90
  601.8 1.6 fusion.92
  606.6 3.5 fusion.88
  610.0 2.7 fusion.89
  613.0 1.5 fusion.90
  615.9 1.6 fusion.92
  620.7 3.5 fusion.88
  624.2 2.7 fusion.89
  627.1 1.5 fusion.90
  630.0 1.6 fusion.92
  634.8 3.5 fusion.88
  638.3 2.7 fusion.89
  641.2 1.5 fusion.90
  644.1 1.6 fusion.92
  648.9 3.5 fusion.88
  652.4 2.7 fusion.89
  655.3 1.5 fusion.90
  658.3 1.6 fusion.92
  663.0 3.5 fusion.88
  666.5 2.7 fusion.89
  669.4 1.5 fusion.90
  672.4 1.6 fusion.92
  677.2 3.5 fusion.88
  680.6 2.7 fusion.89
  683.5 1.5 fusion.90
  686.5 1.6 fusion.92
  691.3 3.5 fusion.88
  694.7 2.7 fusion.89
  697.6 1.5 fusion.90
  700.6 1.6 fusion.92
  705.4 3.5 fusion.88
  708.8 2.7 fusion.89
  711.8 1.5 fusion.90
  714.7 1.6 fusion.92
  719.5 3.5 fusion.88
  723.0 2.7 fusion.89
  725.9 1.5 fusion.90
  728.8 1.6 fusion.92
  734.7 53.4 %all-reduce = f32[768]{0:T(1024)S(1)} all-reduce(f32[768]{0:T(1024)} %get-tuple-element.63), channel_id=3, replica_groups=mesh['enc'=8,'kr'=8,'kc'=4] {'kc'}, use_global_device_ids=true, to_apply=%region_7.8.clone | all-reduce | flops 768 | bytes 6144
  788.3 32.9 %reduce-scatter.8.cloned.1.call-done = f32[192,64]{1,0:T(8,128)} async-done(((f32[768,64]{1,0:T(8,128)}), f32[192,64]{1,0:T(8,128)}) %reduce-scatter.8.cloned.1.call-update) | async-done | bytes 49168
  823.4 4.3 convolution_bitcast_fusion
  827.7 28.4 %reduce-scatter.6.cloned.1.call-done = f32[192,128]{1,0:T(8,128)} async-done(((f32[768,128]{1,0:T(8,128)}), f32[192,128]{1,0:T(8,128)}) %reduce-scatter.6.cloned.1.call-update) | async-done | bytes 98320 | tf_op jit(solution)/shard_map/reduce_scatter | solution.py:43
  856.1 1.5 multiply_convert_fusion.1
  857.6 277.0 %all-reduce.6.cloned.1.call-done = (f32[1024,1024]{0,1:T(8,128)}, f32[1024,64]{1,0:T(8,128)}) async-done(((f32[1024,1024]{0,1:T(8,128)}, f32[1024,64]{1,0:T(8,128)}), (f32[1024,1024]{0,1:T(8,128)}, f32[1024,64]{1,0:T(8,128)})) %all-reduce.6.cloned.1.call-update) | async-done | bytes 4456464
  (169 shorter events, 70.2 us)
Async XLA Ops:
  7.2 1.6 copy-start
  7.2 4.1 copy-start.9
  7.2 4.1 copy-start.10
  7.2 259.8 %all-gather.7.cloned.1.call-start = ((), (), s32[]{:S(2)}) async-start(), calls=%async_computation.5 | async-start | bytes 2129920 | tf_op jit(solution)/shard_map/all_gather | solution.py:72
  8.8 3.4 copy-start.6
  14.6 12.4 %copy-start.4 = (bf16[192,64]{0,1:T(8,128)(2,1)S(1)}, bf16[192,64]{0,1:T(8,128)(2,1)}, u32[]{:S(2)}) copy-start(bf16[192,64]{0,1:T(8,128)(2,1)} %fusion.38) | copy-start | bytes 73732
  14.6 26.9 %copy-start.5 = (bf16[192,128]{1,0:T(8,128)(2,1)S(1)}, bf16[192,128]{1,0:T(8,128)(2,1)}, u32[]{:S(2)}) copy-start(bf16[192,128]{1,0:T(8,128)(2,1)} %param.13) | copy-start | bytes 147460
  14.6 257.1 %all-to-all-start = ((bf16[64,192,128]{2,1,0:T(8,128)(2,1)}), bf16[64,192,128]{2,1,0:T(8,128)(2,1)}, u32[]{:S(2)}, u32[]{:S(2)}) async-start(bf16[64,192,128]{2,1,0:T(8,128)(2,1)} %stack.2), calls=%async_computation | async-start | bytes 6291456 | tf_op jit(solution)/shard_map/all_to_all | solution.py:74
  26.1 536.9 %all-gather.5.cloned.1.call-start = ((), (), s32[]{:S(2)}) async-start(), calls=%async_computation.3 | async-start | bytes 3194880 | tf_op jit(solution)/shard_map/all_gather | solution.py:77
  26.9 794.3 %reduce-scatter.8.cloned.1.call-start = ((), (), s32[]{:S(2)}) async-start(), calls=%async_computation.6 | async-start | bytes 491520
  40.1 0.6 copy-start.3
  563.0 170.4 %copy-start.12 = (u32[256]{0:T(256)S(1)}, u32[256]{0:T(256)}, u32[]{:S(2)}) copy-start(u32[256]{0:T(256)} %constant.36) | copy-start | bytes 3076
  563.1 171.6 %copy-start.11 = (f32[64]{0:T(128)S(1)}, f32[64]{0:T(128)}, u32[]{:S(2)}) copy-start(f32[64]{0:T(128)} %param.11) | copy-start | bytes 772
  567.7 2.9 copy-start.1
  573.6 3.0 copy-start.7
  576.6 0.6 copy-start.8
  581.8 2.9 copy-start.1
  587.7 3.0 copy-start.7
  590.7 0.6 copy-start.8
  595.9 2.9 copy-start.1
  601.8 3.0 copy-start.7
  604.8 0.6 copy-start.8
  610.0 2.9 copy-start.1
  615.9 3.0 copy-start.7
  618.9 0.6 copy-start.8
  624.2 2.9 copy-start.1
  630.0 3.0 copy-start.7
  633.1 0.6 copy-start.8
  638.3 2.9 copy-start.1
  644.1 3.0 copy-start.7
  647.2 0.6 copy-start.8
  652.4 2.9 copy-start.1
  658.2 3.0 copy-start.7
  661.3 0.6 copy-start.8
  666.5 2.9 copy-start.1
  672.4 3.0 copy-start.7
  675.4 0.6 copy-start.8
  680.6 2.9 copy-start.1
  686.5 3.0 copy-start.7
  689.5 0.6 copy-start.8
  694.7 2.9 copy-start.1
  700.6 3.0 copy-start.7
  703.6 0.6 copy-start.8
  708.8 2.9 copy-start.1
  714.7 3.0 copy-start.7
  717.7 0.6 copy-start.8
  723.0 2.9 copy-start.1
  728.8 3.0 copy-start.7
  731.8 0.6 copy-start.8
  732.4 55.7 %copy-start.2 = (f32[768,128]{1,0:T(8,128)}, f32[768,128]{1,0:T(8,128)S(1)}, u32[]{:S(2)}) copy-start(f32[768,128]{1,0:T(8,128)S(1)} %get-tuple-element.62) | copy-start | bytes 1179652
  733.4 122.7 %reduce-scatter.6.cloned.1.call-start = ((), (), s32[]{:S(2)}) async-start(), calls=%async_computation.4 | async-start | bytes 491520 | tf_op jit(solution)/shard_map/reduce_scatter | solution.py:43
  788.2 346.5 %all-reduce.6.cloned.1.call-start = ((), (), s32[]{:S(2)}) async-start(), calls=%async_computation.7 | async-start | bytes 9437184
Sparse Core Ops, SparseCore 0:
  12.3 254.7 all-gather.6
  268.8 294.1 all-gather.4
  733.5 87.6 reduce-scatter.7
  823.8 32.2 reduce-scatter.5
  861.5 273.0 all-reduce.5
